TPU v7x, 512 devices: a whole 4x4x16 slice. The times are simulated.
512 devices in a mesh: expert: 32 (over z, core), tensor: 16 (over y, x).
Axes of the slice: x: 4, y: 4, z: 16, core: 2. Of those that a mesh axis runs over, the one named last changes fastest.
Arguments:
- hidden_in: bfloat16 [4096, 4096], P('expert', 'tensor'), may hold values from -92 to 92
- norm_gain: float32 [4096], P('tensor'), may hold values from 0.5 to 1.5
- expert_ids: int32 [4096, 8], P('expert'), may hold values from 0 to 63, all different within a row; in each aligned block of 128 rows (0 to 127, 128 to 255, ...) at most 24 rows name the same one
- route_weights: float32 [4096, 8], P('expert'), may hold values from 0.05 to 0.5
- w_gate: bfloat16 [64, 1536, 4096], P('expert', 'tensor'), may hold values from -0.09375 to 0.09375
- w_up: bfloat16 [64, 1536, 4096], P('expert', 'tensor'), may hold values from -0.09375 to 0.09375
- w_down: bfloat16 [64, 1536, 4096], P('expert', 'tensor'), may hold values from -0.15625 to 0.15625
Outputs:
- moe_out: bfloat16 [4096, 4096], P('expert', 'tensor')
Inputs may be any that keep to these rules, and one draw needn't show every extreme that they name: `expert_ids`: in each aligned block of 128 rows (the rows of one index of the expert axis) no expert is named by more than 24 rows, a bound that some block reaches.
All inputs are finite; a program needn't handle non-finite values.
Results may differ from a plain program's by a relative error of at most 0.019.
Values may be sent and summed in bfloat16 or wider, within the bound.
A program may use at most 128 MiB of HBM per device.

v0:
```python
import jax
import jax.numpy as jnp
from jax import lax
from jax.sharding import PartitionSpec as P

D = 4096
epsilon = 1e-06


def body(hidden_in, norm_gain, expert_ids, route_weights, w_gate, w_up, w_down):
    tokens_here = hidden_in.shape[0]
    choices_count = expert_ids.shape[1]
    exp_local = w_gate.shape[0]
    groups = lax.axis_size("expert")
    experts_all = exp_local * groups
    capacity = min(tokens_here, 3 * tokens_here * choices_count // (2 * experts_all))
    widened = hidden_in.astype(jnp.float32)
    squares = lax.psum(jnp.sum(widened * widened, axis=1), "tensor")
    normed = (widened * lax.rsqrt(squares / D + epsilon)[:, None] * norm_gain[None, :]).astype(
        jnp.bfloat16
    )
    routing = jnp.concatenate([expert_ids.astype(jnp.float32), route_weights], axis=1)
    routing = lax.all_gather(routing.T, "expert", axis=0, tiled=False)
    tokens_all = lax.all_gather(normed, "expert", axis=0, tiled=False)
    first = (lax.axis_index("expert") * exp_local).astype(jnp.float32)
    named = (
        routing[:, None, :choices_count, :]
        == first + jnp.arange(exp_local, dtype=jnp.float32)[None, :, None, None]
    )
    chosen = jnp.any(named, axis=2)
    scale = jnp.sum(jnp.where(named, routing[:, None, choices_count:, :], 0.0), axis=2)
    step = jnp.arange(tokens_here, dtype=jnp.int32)
    earlier = (step[:, None] < step[None, :]).astype(jnp.bfloat16)
    position = jnp.einsum(
        "bjs,st->bjt", chosen.astype(jnp.bfloat16), earlier, preferred_element_type=jnp.float32
    )
    slot = jnp.arange(capacity, dtype=jnp.float32)
    select = (
        (position[:, :, None, :] == slot[None, None, :, None]) & chosen[:, :, None, :]
    ).astype(jnp.bfloat16)
    rows = jnp.einsum(
        "bjst,btd->bjsd", select, tokens_all, preferred_element_type=jnp.float32
    ).astype(jnp.bfloat16)
    rows = rows.transpose(1, 0, 2, 3).reshape(exp_local, groups * capacity, -1)
    piece = lax.all_gather(rows, "tensor", axis=2, tiled=True)
    gate_add = jnp.einsum("erd,efd->erf", piece, w_gate, preferred_element_type=jnp.float32)
    up_add = jnp.einsum("erd,efd->erf", piece, w_up, preferred_element_type=jnp.float32)
    inner = (jax.nn.silu(gate_add) * up_add).astype(jnp.bfloat16)
    partials = jnp.einsum("erf,efd->erd", inner, w_down, preferred_element_type=jnp.float32).astype(
        jnp.bfloat16
    )
    summed = lax.psum_scatter(partials, "tensor", scatter_dimension=2, tiled=True)
    summed = summed.reshape(exp_local, groups, capacity, -1)
    back = jnp.einsum("bjst,jbsd->bjtd", select, summed, preferred_element_type=jnp.float32)
    weighted = jnp.sum(back * scale[:, :, :, None], axis=1).astype(jnp.bfloat16)
    return lax.psum_scatter(weighted, "expert", scatter_dimension=0, tiled=False)


def solution(mesh):
    placed = (
        P("expert", "tensor"),
        P("tensor"),
        P("expert", None),
        P("expert", None),
        P("expert", "tensor", None),
        P("expert", "tensor", None),
        P("expert", "tensor", None),
    )
    return jax.shard_map(
        body, mesh=mesh, in_specs=placed, out_specs=P("expert", "tensor"), check_vma=False
    )
```

profile of v0, /device:TPU:18, one launch (start us, length us, event | category | flops | bytes accessed | tf_op | source)
XLA Modules:
  0.0 491.3 jit_solution(8719006843433217021)
XLA Ops:
  6.5 1.1 fusion.17
  7.6 31.1 %psum.7 = f32[128]{0:T(128)S(1)} all-reduce(f32[128]{0:T(128)S(1)} %fusion.17), channel_id=1, replica_groups=mesh['expert'=32,'tensor'=16] {'tensor'}, use_global_device_ids=true, to_apply=%region_2.0 | all-reduce | flops 128 | bytes 1024 | tf_op jit(solution)/shard_map/psum | solution.py:18
  38.8 1.6 fusion.19
  40.3 0.0 all-gather.7.cloned.1.call-update
  40.3 0.0 all-gather.5.cloned.1.call-start
  40.4 0.7 convert_element_type.31
  41.1 0.7 maximum_bitcast_fusion
  41.8 37.0 %all-gather = f32[512,128]{1,0:T(8,128)S(1)} all-gather(f32[16,128]{1,0:T(8,128)S(1)} %maximum_bitcast_fusion), channel_id=2, replica_groups=mesh['expert'=32,'tensor'=16] {'expert'}, dimensions={0}, use_global_device_ids=true | all-gather | bytes 270336 | tf_op jit(solution)/shard_map/all_gather | solution.py:23
  78.8 0.2 compare_reduce_fusion
  79.0 0.1 fusion.21
  79.2 41.8 %all-gather.7.cloned.1.call-done = bf16[4096,256]{1,0:T(8,128)(2,1)} async-done(((bf16[128,256]{1,0:T(8,128)(2,1)}), bf16[4096,256]{1,0:T(8,128)(2,1)}) %all-gather.7.cloned.1.call-update) | async-done | bytes 2097168 | tf_op jit(solution)/shard_map/all_gather | solution.py:24
  121.0 2.0 fusion
  123.0 1.0 copy.17
  124.0 0.0 all-gather.5.cloned.1.call-update
  124.0 0.0 reduce-scatter.3.cloned.1.call-start
  124.1 110.4 %all-gather.5.cloned.1.call-done = bf16[2,768,4096]{2,1,0:T(8,128)(2,1)} async-done(((bf16[2,768,256]{2,1,0:T(8,128)(2,1)}), bf16[2,768,4096]{2,1,0:T(8,128)(2,1)}) %all-gather.5.cloned.1.call-update) | async-done | bytes 12582928 | tf_op jit(solution)/shard_map/all_gather | solution.py:45
  234.4 9.0 %fusion.26 = f32[2,768,96]{1,2,0:T(8,128)S(1)} fusion(bf16[2,768,4096]{2,1,0:T(8,128)(2,1)} %all-gather.5.cloned.1.call-done, bf16[2,96,4096]{2,1,0:T(8,128)(2,1)} %param.11), kind=kOutput, calls=%fused_computation.36 | convolution fusion | flops 1207959552 | bytes 14745600 | tf_op jit(solution)/shard_map/erd,efd->erf/dot_general | solution.py:46
  243.4 15.3 %convolution_convert_fusion = bf16[2,768,4096]{2,1,0:T(8,128)(2,1)} fusion(bf16[2,96,4096]{2,1,0:T(8,128)(2,1)S(1)} %copy-done, bf16[2,768,4096]{2,1,0:T(8,128)(2,1)} %all-gather.5.cloned.1.call-done, bf16[2,96,4096]{2,1,0:T(8,128)(2,1)} %param.12, f32[2,768,96]{1,2,0:T(8,128)S(1)} %fusion.26), kind=kOutput, calls=%fused_computation | convolution fusion | flops 2423095296 | bytes 28901376 | tf_op jit(solution)/shard_map/erf,efd->erd/dot_general | solution.py:49
  258.7 0.0 reduce-scatter.3.cloned.1.call-update
  258.8 0.0 reduce-scatter.5.cloned.1.call-start
  258.8 0.2 fusion.16
  259.0 109.0 %reduce-scatter.3.cloned.1.call-done = bf16[2,768,256]{2,1,0:T(8,128)(2,1)} async-done(((bf16[2,768,4096]{2,1,0:T(8,128)(2,1)}), bf16[2,768,256]{2,1,0:T(8,128)(2,1)}) %reduce-scatter.3.cloned.1.call-update) | async-done | bytes 786448 | tf_op jit(solution)/shard_map/reduce_scatter | solution.py:52
  368.0 5.3 %multiply_reduce_fusion = bf16[32,128,256]{2,1,0:T(8,128)(2,1)} fusion(f32[32,2,128]{2,1,0:T(2,128)S(1)} %fusion.16, bf16[2,32,24,256]{3,2,1,0:T(8,128)(2,1)} %bitcast.25, f32[32,2,128]{2,1,0:T(2,128)S(1)} %copy.16, pred[32,2,128]{2,1,0:T(4,128)(4,1)S(1)} %compare_reduce_fusion), kind=kOutput, calls=%fused_computation.1 | convolution fusion | flops 104202240 | bytes 2957312 | tf_op jit(solution)/shard_map/bjst,jbsd->bjtd/dot_general | solution.py:54
  373.3 111.5 %reduce-scatter.5.cloned.1.call-done = bf16[1,128,256]{2,1,0:T(8,128)(2,1)} async-done(((bf16[32,128,256]{2,1,0:T(8,128)(2,1)}), bf16[1,128,256]{2,1,0:T(8,128)(2,1)}) %reduce-scatter.5.cloned.1.call-update) | async-done | bytes 65552 | tf_op jit(solution)/shard_map/reduce_scatter | solution.py:56
  (8 shorter events, 0.1 us)
Async XLA Ops:
  6.5 236.9 %copy-start = (bf16[2,96,4096]{2,1,0:T(8,128)(2,1)S(1)}, bf16[2,96,4096]{2,1,0:T(8,128)(2,1)}, u32[]{:S(2)}) copy-start(bf16[2,96,4096]{2,1,0:T(8,128)(2,1)} %param.13) | copy-start | bytes 4718596
  6.5 114.5 %all-gather.7.cloned.1.call-start = ((), (), s32[]{:S(2)}) async-start(), calls=%async_computation.5 | async-start | bytes 2162688 | tf_op jit(solution)/shard_map/all_gather | solution.py:24
  40.3 194.1 %all-gather.5.cloned.1.call-start = ((), (), s32[]{:S(2)}) async-start(), calls=%async_computation.2 | async-start | bytes 13369344 | tf_op jit(solution)/shard_map/all_gather | solution.py:45
  124.0 243.9 %reduce-scatter.3.cloned.1.call-start = ((), (), s32[]{:S(2)}) async-start(), calls=%async_computation.3 | async-start | bytes 13369344 | tf_op jit(solution)/shard_map/reduce_scatter | solution.py:52
  258.8 226.0 %reduce-scatter.5.cloned.1.call-start = ((), (), s32[]{:S(2)}) async-start(), calls=%async_computation.4 | async-start | bytes 2162688 | tf_op jit(solution)/shard_map/reduce_scatter | solution.py:56
Sparse Core Ops, SparseCore 0:
  40.5 80.4 all-gather.6
  124.1 110.2 all-gather.4
  258.9 109.0 reduce-scatter.2
  373.4 111.3 reduce-scatter.4
where the time goes:
time: 492 us; the launch traced here: 491 us
  waiting for transfers between devices  373 us (76%)
  blocking collectives  68.2 us (14%)
  matrix products  31.7 us (6%)
  between operations  13.2 us (3%)
    reduce_scatter x1, waiting for transfers between devices, body(): lax.psum_scatter(weighted, 'expert', scatter_dimension=0, tiled=False)  111 us
    all_gather x1, waiting for transfers between devices, body(): piece = lax.all_gather(rows, 'tensor', axis=2, tiled=True)  110 us
    reduce_scatter x1, waiting for transfers between devices, body(): lax.psum_scatter(partials, 'tensor', scatter_dimension=2, tiled=True)  109 us
    all_gather x1, waiting for transfers between devices, body(): tokens_all = lax.all_gather(normed, 'expert', axis=0, tiled=False)  41.8 us
    all_gather x1, blocking collectives, body(): routing = lax.all_gather(routing.T, 'expert', axis=0, tiled=False)  37 us
    psum x1, blocking collectives, body(): squares = lax.psum(jnp.sum(widened * widened, axis=1), 'tensor')  31.1 us
    dot_general x1, matrix products, body(): jnp.einsum('erf,efd->erd', inner, w_down, preferred_element_type=jnp.floa...  15.3 us
  transfers between devices with their start and end apart: 4, of which 4 were waited for; matrix products, arithmetic and copies ran while one was open for 0% of the time, Pallas kernels for 0%

commit v1 on v0

--- a/solution.py
+++ b/solution.py
@@ -5,6 +5,11 @@
 
 D = 4096
 epsilon = 1e-06
+
+
+def gather_over(array, mesh_axis, along):
+    sent = jnp.stack([array] * lax.axis_size(mesh_axis))
+    return jnp.concatenate(lax.all_to_all(sent, mesh_axis, 0, 0), axis=along)
 
 
 def body(hidden_in, norm_gain, expert_ids, route_weights, w_gate, w_up, w_down):
@@ -42,7 +47,7 @@
         "bjst,btd->bjsd", select, tokens_all, preferred_element_type=jnp.float32
     ).astype(jnp.bfloat16)
     rows = rows.transpose(1, 0, 2, 3).reshape(exp_local, groups * capacity, -1)
-    piece = lax.all_gather(rows, "tensor", axis=2, tiled=True)
+    piece = gather_over(rows, "tensor", 2)
     gate_add = jnp.einsum("erd,efd->erf", piece, w_gate, preferred_element_type=jnp.float32)
     up_add = jnp.einsum("erd,efd->erf", piece, w_up, preferred_element_type=jnp.float32)
     inner = (jax.nn.silu(gate_add) * up_add).astype(jnp.bfloat16)

time: 492 us -> 532 us (1.081)
  the two profiles are of different devices: /device:TPU:18 before, /device:TPU:2 now
where the time goes in v1:
time: 532 us
  waiting for transfers between devices  250 us (47%)
  blocking collectives  221 us (42%)
  matrix products  31.8 us (6%)
  between operations  13.2 us (2%)
  local copies, waits for them, and re-layouts  11.5 us (2%)
    all_to_all x1, blocking collectives, gather_over(): return jnp.concatenate(lax.all_to_all(sent, mesh_axis, 0, 0), axis=along)  147 us
    reduce_scatter x1, waiting for transfers between devices, body(): lax.psum_scatter(weighted, 'expert', scatter_dimension=0, tiled=False)  110 us
    reduce_scatter x1, waiting for transfers between devices, body(): lax.psum_scatter(partials, 'tensor', scatter_dimension=2, tiled=True)  103 us
    psum x1, blocking collectives, body(): squares = lax.psum(jnp.sum(widened * widened, axis=1), 'tensor')  41.4 us
    all_gather x1, waiting for transfers between devices, body(): tokens_all = lax.all_gather(normed, 'expert', axis=0, tiled=False)  36.6 us
    all_gather x1, blocking collectives, body(): routing = lax.all_gather(routing.T, 'expert', axis=0, tiled=False)  32.2 us
    dot_general x1, matrix products, body(): jnp.einsum('erf,efd->erd', inner, w_down, preferred_element_type=jnp.floa...  15.4 us
  transfers between devices with their start and end apart: 3, of which 3 were waited for; matrix products, arithmetic and copies ran while one was open for 0% of the time, Pallas kernels for 0%

profile of v1, /device:TPU:2, one launch (start us, length us, event | category | flops | bytes accessed | tf_op | source)
XLA Modules:
  0.0 531.6 jit_solution(8178726972316484265)
XLA Ops:
  6.5 1.1 fusion.17
  7.6 41.4 %psum.7 = f32[128]{0:T(128)S(1)} all-reduce(f32[128]{0:T(128)S(1)} %fusion.17), channel_id=1, replica_groups=mesh['expert'=32,'tensor'=16] {'tensor'}, use_global_device_ids=true, to_apply=%region_2.0 | all-reduce | flops 128 | bytes 1024 | tf_op jit(solution)/shard_map/psum | solution.py:23
  49.0 1.6 fusion.19
  50.6 0.0 reduce-scatter.3.cloned.1.call-start
  50.6 0.7 convert_element_type.31
  51.3 0.7 maximum_bitcast_fusion
  52.0 32.2 %all-gather = f32[512,128]{1,0:T(8,128)S(1)} all-gather(f32[16,128]{1,0:T(8,128)S(1)} %maximum_bitcast_fusion), channel_id=2, replica_groups=mesh['expert'=32,'tensor'=16] {'expert'}, dimensions={0}, use_global_device_ids=true | all-gather | bytes 270336 | tf_op jit(solution)/shard_map/all_gather | solution.py:28
  84.3 0.2 compare_reduce_fusion
  84.4 0.1 fusion.21
  84.6 36.6 %all-gather.4.cloned.1.call-done = bf16[4096,256]{1,0:T(8,128)(2,1)} async-done(((bf16[128,256]{1,0:T(8,128)(2,1)}), bf16[4096,256]{1,0:T(8,128)(2,1)}) %all-gather.4.cloned.1.call-update) | async-done | bytes 2097168 | tf_op jit(solution)/shard_map/all_gather | solution.py:29
  121.2 2.0 fusion
  123.2 0.1 copy.22
  123.3 6.0 %stack.3 = bf16[16,2,768,256]{3,2,1,0:T(8,128)(2,1)} broadcast(bf16[2,768,256]{2,1,0:T(8,128)(2,1)S(1)} %bitcast.28), dimensions={1,2,3} | broadcast | bytes 13369344 | tf_op jit(solution)/shard_map/stack | solution.py:11
  129.3 147.0 %all_to_all.5 = bf16[16,2,768,256]{3,2,1,0:T(8,128)(2,1)S(1)} all-to-all(bf16[16,2,768,256]{3,2,1,0:T(8,128)(2,1)} %stack.3), channel_id=1, replica_groups=mesh['expert'=32,'tensor'=16] {'tensor'}, dimensions={0} | all-to-all | bytes 25165824 | tf_op jit(solution)/shard_map/all_to_all | solution.py:12
  276.3 5.4 %copy.26 = bf16[16,2,96,8,256]{4,3,0,2,1:T(8,128)(2,1)} copy(bf16[16,2,96,8,256]{4,3,2,1,0:T(8,128)(2,1)S(1)} %bitcast.27) | data formatting | bytes 25165824 | tf_op jit(solution)/shard_map/reshape | solution.py:12
  281.7 9.0 %fusion.26 = f32[2,768,96]{1,2,0:T(8,128)S(1)} fusion(bf16[2,768,4096]{2,1,0:T(8,128)(2,1)} %bitcast.25, bf16[2,96,4096]{2,1,0:T(8,128)(2,1)} %param.11), kind=kOutput, calls=%fused_computation.36 | convolution fusion | flops 1207959552 | bytes 14745600 | tf_op jit(solution)/shard_map/erd,efd->erf/dot_general | solution.py:51
  290.7 15.4 %convolution_convert_fusion = bf16[2,768,4096]{2,1,0:T(8,128)(2,1)} fusion(bf16[2,96,4096]{2,1,0:T(8,128)(2,1)S(1)} %copy-done, bf16[2,768,4096]{2,1,0:T(8,128)(2,1)} %bitcast.26, bf16[2,96,4096]{2,1,0:T(8,128)(2,1)} %param.12, f32[2,768,96]{1,2,0:T(8,128)S(1)} %fusion.26), kind=kOutput, calls=%fused_computation | convolution fusion | flops 2423095296 | bytes 28901376 | tf_op jit(solution)/shard_map/erf,efd->erd/dot_general | solution.py:54
  306.1 0.0 reduce-scatter.3.cloned.1.call-update
  306.1 0.0 reduce-scatter.5.cloned.1.call-start
  306.2 0.2 fusion.16
  306.3 103.4 %reduce-scatter.3.cloned.1.call-done = bf16[2,768,256]{2,1,0:T(8,128)(2,1)} async-done(((bf16[2,768,4096]{2,1,0:T(8,128)(2,1)}), bf16[2,768,256]{2,1,0:T(8,128)(2,1)}) %reduce-scatter.3.cloned.1.call-update) | async-done | bytes 786448 | tf_op jit(solution)/shard_map/reduce_scatter | solution.py:57
  409.7 5.3 multiply_reduce_fusion
  415.0 0.0 reduce-scatter.5.cloned.1.call-update
  415.1 110.0 %reduce-scatter.5.cloned.1.call-done = bf16[1,128,256]{2,1,0:T(8,128)(2,1)} async-done(((bf16[32,128,256]{2,1,0:T(8,128)(2,1)}), bf16[1,128,256]{2,1,0:T(8,128)(2,1)}) %reduce-scatter.5.cloned.1.call-update) | async-done | bytes 65552 | tf_op jit(solution)/shard_map/reduce_scatter | solution.py:61
  (8 shorter events, 0.1 us)
Async XLA Ops:
  6.5 284.2 %copy-start = (bf16[2,96,4096]{2,1,0:T(8,128)(2,1)S(1)}, bf16[2,96,4096]{2,1,0:T(8,128)(2,1)}, u32[]{:S(2)}) copy-start(bf16[2,96,4096]{2,1,0:T(8,128)(2,1)} %param.13) | copy-start | bytes 4718596
  6.5 114.7 %all-gather.4.cloned.1.call-start = ((), (), s32[]{:S(2)}) async-start(), calls=%async_computation.5 | async-start | bytes 2162688 | tf_op jit(solution)/shard_map/all_gather | solution.py:29
  50.6 359.2 %reduce-scatter.3.cloned.1.call-start = ((), (), s32[]{:S(2)}) async-start(), calls=%async_computation.3 | async-start | bytes 13369344 | tf_op jit(solution)/shard_map/reduce_scatter | solution.py:57
  306.1 218.9 %reduce-scatter.5.cloned.1.call-start = ((), (), s32[]{:S(2)}) async-start(), calls=%async_computation.4 | async-start | bytes 2162688 | tf_op jit(solution)/shard_map/reduce_scatter | solution.py:61
Sparse Core Ops, SparseCore 0:
  50.7 70.4 all-gather.3
  306.2 103.4 reduce-scatter.2
  415.2 109.8 reduce-scatter.4
